TPU v7x, 128 devices: a whole 4x4x4 slice. The times are simulated.
128 devices in a mesh: section: 2 (over x_hi), dp: 8 (over z, core), mp: 8 (over x_lo, y).
Axes of the slice: x: 4 (x_hi: 2, x_lo: 2; x = x_hi * 2 + x_lo), y: 4, z: 4, core: 2. Of those that a mesh axis runs over, the one named last changes fastest.
Arguments:
- inputs: bfloat16 [2, 16, 128, 4096], P('section', 'dp'), may hold values from -6 to 6
- norm_gains: bfloat16 [2, 4096], P('section'), may hold values from 0.5 to 1.5
- weights: bfloat16 [2, 4096, 4, 4096], P('section', 'dp', None, 'mp'), may hold values from -0.09375 to 0.09375
- cotangent: bfloat16 [16, 128, 4096], P('dp'), may hold values from -6 to 6
- lengths: int32 [2, 16], P(None, 'dp'), may hold values from 32 to 128, as said below
- dp_noise: float32 [2, 4096, 4, 4096], P('section', 'dp', None, 'mp'), may hold values from -6 to 6
Outputs:
- noisy_grad: float32 [2, 4096, 4, 4096], P('section', 'dp', None, 'mp')
- clip_scale: float32 [16], P('dp')
Inputs may be any that keep to these rules, and one draw needn't show every extreme that they name: `lengths`: the first example of each row has length 128.
All inputs are finite; a program needn't handle non-finite values.
Results may differ from a plain program's by a relative error of at most 0.024.
Values may be sent and summed in bfloat16 or wider, within the bound.
A program may use at most 256 MiB of HBM per device.

v0:
```python
import jax
import jax.numpy as jnp
from jax import lax
from jax.sharding import PartitionSpec as P

D = 4096
HEADS = 64
HEAD = 64


def from_partner(x, axis, distance):
    return lax.ppermute(x, axis, [(i, i ^ 1 << distance) for i in range(lax.axis_size(axis))])


def rms_norm(values_in, gain_row):
    value32 = values_in.astype(jnp.float32)
    inverse = lax.rsqrt(jnp.mean(value32 * value32, axis=-1, keepdims=True) + 1e-06)
    return (value32 * inverse * gain_row.astype(jnp.float32)).astype(jnp.bfloat16)


def project(left, right):
    return jnp.dot(left, right, preferred_element_type=jnp.float32).astype(jnp.bfloat16)


def attend(queries, key_proj, value_proj, key_mask):
    seq_len = queries.shape[0]
    query_heads = queries.reshape(seq_len, -1, HEAD)
    key_heads = key_proj.reshape(seq_len, -1, HEAD)
    value_heads = value_proj.reshape(seq_len, -1, HEAD)
    scores = jnp.einsum(
        "shd,thd->hst", query_heads, key_heads, preferred_element_type=jnp.float32
    ) * HEAD ** (-0.5)
    scores = jnp.where(key_mask[None, None, :], scores, -jnp.inf)
    attn_probs = jax.nn.softmax(scores, axis=-1)
    probs_low = attn_probs.astype(jnp.bfloat16)
    context = jnp.einsum("hst,thd->shd", probs_low, value_heads, preferred_element_type=jnp.float32)
    return (attn_probs, context.reshape(seq_len, -1).astype(jnp.bfloat16))


def attend_back(queries, key_proj, value_proj, attn_probs, grad_ctx):
    seq_len = queries.shape[0]
    query_heads = queries.reshape(seq_len, -1, HEAD)
    key_heads = key_proj.reshape(seq_len, -1, HEAD)
    value_heads = value_proj.reshape(seq_len, -1, HEAD)
    grad_heads = grad_ctx.reshape(seq_len, -1, HEAD)
    grad_probs = jnp.einsum(
        "shd,thd->hst", grad_heads, value_heads, preferred_element_type=jnp.float32
    )
    inner_sum = jnp.sum(grad_probs * attn_probs, axis=-1, keepdims=True)
    grad_scores = (attn_probs * (grad_probs - inner_sum) * HEAD ** (-0.5)).astype(jnp.bfloat16)
    probs_low = attn_probs.astype(jnp.bfloat16)
    grad_query = jnp.einsum(
        "hst,thd->shd", grad_scores, key_heads, preferred_element_type=jnp.float32
    )
    grad_key = jnp.einsum(
        "hst,shd->thd", grad_scores, query_heads, preferred_element_type=jnp.float32
    )
    grad_value = jnp.einsum(
        "hst,shd->thd", probs_low, grad_heads, preferred_element_type=jnp.float32
    )
    return (
        grad_query.reshape(seq_len, -1).astype(jnp.bfloat16),
        grad_key.reshape(seq_len, -1).astype(jnp.bfloat16),
        grad_value.reshape(seq_len, -1).astype(jnp.bfloat16),
    )


def gram(matrix):
    return jnp.dot(matrix, matrix.T, preferred_element_type=jnp.float32)


def ghost(normed, kv_rows, grad_query, grad_key, grad_value, grad_out, context):
    first = jnp.sum(gram(normed) * gram(grad_query))
    second = jnp.sum(gram(kv_rows) * (gram(grad_key) + gram(grad_value)))
    third = jnp.sum(gram(grad_out) * gram(context))
    return first + second + third


def get_row(buffer, index):
    return lax.dynamic_index_in_dim(buffer, index, 0, keepdims=False)


def put_row(buffer, value, index, valid):
    current = get_row(buffer, index)
    return lax.dynamic_update_index_in_dim(buffer, jnp.where(valid, value, current), index, 0)


def per_device(inputs, norm_gains, weights, cotangent, lengths, dp_noise):
    section_index = lax.axis_index("section")
    is_dec = section_index == 1
    micro_count = inputs.shape[1]
    seq_len = inputs.shape[2]
    width = inputs.shape[3]
    gathered = lax.all_gather(weights, "dp", axis=1, tiled=True)[0]
    inner_dev = gathered.shape[2]
    own_inputs = inputs[0]
    gain_row = norm_gains[0]
    positions = jnp.arange(seq_len)
    wide_zero = jnp.zeros((micro_count, seq_len, width), jnp.bfloat16)
    thin_zero = jnp.zeros((micro_count, seq_len, inner_dev), jnp.bfloat16)
    normed_buf, kv_buf, gout_buf = (wide_zero, wide_zero, wide_zero)
    query_buf, key_buf, value_buf, context_buf = (thin_zero, thin_zero, thin_zero, thin_zero)
    gq_buf, gk_buf, gv_buf = (thin_zero, thin_zero, thin_zero)
    probs_buf = jnp.zeros((micro_count, inner_dev // HEAD, seq_len, seq_len), jnp.float32)
    norm_parts = jnp.zeros((micro_count,), jnp.float32)
    incoming = jnp.zeros((seq_len, width), jnp.bfloat16)
    for step_num in range(micro_count + 2):
        fwd_mb = step_num - section_index
        fwd_ok = (fwd_mb >= 0) & (fwd_mb < micro_count)
        fwd_idx = jnp.clip(fwd_mb, 0, micro_count - 1)
        rows_now = get_row(own_inputs, fwd_idx)
        normed = rms_norm(rows_now, gain_row)
        kv_rows = jnp.where(is_dec, incoming, normed)
        queries = project(normed, gathered[:, 0])
        key_proj = project(kv_rows, gathered[:, 1])
        value_proj = project(kv_rows, gathered[:, 2])
        key_mask = positions < get_row(lengths[0], fwd_idx)
        attn_probs, context_new = attend(queries, key_proj, value_proj, key_mask)
        normed_buf = put_row(normed_buf, normed, fwd_idx, fwd_ok)
        kv_buf = put_row(kv_buf, kv_rows, fwd_idx, fwd_ok)
        query_buf = put_row(query_buf, queries, fwd_idx, fwd_ok)
        key_buf = put_row(key_buf, key_proj, fwd_idx, fwd_ok)
        value_buf = put_row(value_buf, value_proj, fwd_idx, fwd_ok)
        probs_buf = put_row(probs_buf, attn_probs, fwd_idx, fwd_ok)
        context_buf = put_row(context_buf, context_new, fwd_idx, fwd_ok)
        bwd_mb = step_num - 2 + section_index
        bwd_ok = (bwd_mb >= 0) & (bwd_mb < micro_count)
        bwd_idx = jnp.clip(bwd_mb, 0, micro_count - 1)
        dec_mask = (positions < get_row(lengths[1], bwd_idx)).astype(jnp.bfloat16)
        cot_rows = get_row(cotangent, bwd_idx) * dec_mask[:, None]
        grad_out = jnp.where(is_dec, cot_rows, incoming)
        grad_ctx = project(grad_out, gathered[:, 3])
        back_query = get_row(query_buf, bwd_idx)
        back_key = get_row(key_buf, bwd_idx)
        back_value = get_row(value_buf, bwd_idx)
        back_context = get_row(context_buf, bwd_idx)
        grad_query, grad_key, grad_value = attend_back(
            back_query, back_key, back_value, get_row(probs_buf, bwd_idx), grad_ctx
        )
        sq_part = ghost(
            get_row(normed_buf, bwd_idx),
            get_row(kv_buf, bwd_idx),
            grad_query,
            grad_key,
            grad_value,
            grad_out,
            back_context,
        )
        gout_buf = put_row(gout_buf, grad_out, bwd_idx, bwd_ok)
        gq_buf = put_row(gq_buf, grad_query, bwd_idx, bwd_ok)
        gk_buf = put_row(gk_buf, grad_key, bwd_idx, bwd_ok)
        gv_buf = put_row(gv_buf, grad_value, bwd_idx, bwd_ok)
        slot_hit = bwd_ok & (jnp.arange(micro_count) == bwd_idx)
        norm_parts = jnp.where(slot_hit, sq_part, norm_parts)
        if step_num < micro_count + 1:
            relay_term = lax.cond(
                is_dec,
                lambda: jnp.einsum(
                    "sj,dj->sd", grad_key, gathered[:, 1], preferred_element_type=jnp.float32
                )
                + jnp.einsum(
                    "sj,dj->sd", grad_value, gathered[:, 2], preferred_element_type=jnp.float32
                ),
                lambda: jnp.einsum(
                    "sj,dj->sd", context_new, gathered[:, 3], preferred_element_type=jnp.float32
                ),
            )
            residual = jnp.where(is_dec, 0.0, rows_now.astype(jnp.float32))
            summed_rows = lax.psum(relay_term.astype(jnp.bfloat16), "mp").astype(jnp.float32)
            payload = (summed_rows + residual).astype(jnp.bfloat16)
            incoming = from_partner(payload, "section", 0)
    sq_norm = lax.psum(norm_parts, ("section", "mp"))
    bound = jnp.sqrt(jnp.float32(8.0 * D * HEADS * HEAD))
    clip_scale = bound / (jnp.sqrt(sq_norm) + 0.01 * bound)
    totals = jnp.zeros((weights.shape[1] * lax.axis_size("dp"), 4, inner_dev), jnp.float32)
    for micro_num in range(micro_count):
        normed_cols = normed_buf[micro_num]
        kv_cols = kv_buf[micro_num]
        gout_cols = gout_buf[micro_num]
        stacked = jnp.stack(
            [
                jnp.einsum(
                    "sd,sj->dj", normed_cols, gq_buf[micro_num], preferred_element_type=jnp.float32
                ),
                jnp.einsum(
                    "sd,sj->dj", kv_cols, gk_buf[micro_num], preferred_element_type=jnp.float32
                ),
                jnp.einsum(
                    "sd,sj->dj", kv_cols, gv_buf[micro_num], preferred_element_type=jnp.float32
                ),
                jnp.einsum(
                    "sd,sj->dj",
                    gout_cols,
                    context_buf[micro_num],
                    preferred_element_type=jnp.float32,
                ),
            ],
            axis=1,
        )
        totals = totals + clip_scale[micro_num] * stacked
    summed = lax.psum_scatter(
        totals.astype(jnp.bfloat16), "dp", scatter_dimension=0, tiled=True
    ).astype(jnp.float32)
    examples_total = micro_count * lax.axis_size("dp")
    noisy_grad = (summed + dp_noise[0]) / examples_total
    return (noisy_grad[None], clip_scale)


def solution(mesh):
    placed = (
        P("section", "dp", None, None),
        P("section", None),
        P("section", "dp", None, "mp"),
        P("dp", None, None),
        P(None, "dp"),
        P("section", "dp", None, "mp"),
    )
    return jax.shard_map(
        per_device,
        mesh=mesh,
        in_specs=placed,
        out_specs=(P("section", "dp", None, "mp"), P("dp")),
        check_vma=False,
    )
```

profile of v0, /device:TPU:1, one launch (start us, length us, event | category | flops | bytes accessed | tf_op | source)
XLA Modules:
  0.0 845.7 jit_solution(15828079697014097432)
XLA Ops:
  38.8 60.7 %all-gather.2.cloned.1.call-done = bf16[1,4096,4,512]{3,1,2,0:T(8,128)(2,1)} async-done(((bf16[1,512,4,512]{3,1,2,0:T(8,128)(2,1)}), bf16[1,4096,4,512]{3,1,2,0:T(8,128)(2,1)}) %all-gather.2.cloned.1.call-update) | async-done | bytes 16777232 | tf_op jit(solution)/shard_map/all_gather | solution.py:94
  130.8 4.8 conditional.3
  130.8 4.8 fusion
  148.2 63.0 %all-reduce.4.cloned.1.call-done = bf16[128,4096]{1,0:T(8,128)(2,1)} async-done(((bf16[128,4096]{1,0:T(8,128)(2,1)}), bf16[128,4096]{1,0:T(8,128)(2,1)}) %all-reduce.4.cloned.1.call-update) | async-done | bytes 1048592 | tf_op jit(solution)/shard_map/psum | solution.py:169
  245.4 6.0 bitcast_dynamic-update-slice_fusion.5
  299.0 4.9 conditional.4
  315.2 70.6 %all-reduce.6.cloned.1.call-done = bf16[128,4096]{1,0:T(8,128)(2,1)} async-done(((bf16[128,4096]{1,0:T(8,128)(2,1)}), bf16[128,4096]{1,0:T(8,128)(2,1)}) %all-reduce.6.cloned.1.call-update) | async-done | bytes 1048592 | tf_op jit(solution)/shard_map/psum | solution.py:169
  395.2 12.4 %collective-permute-done.1 = bf16[128,4096]{1,0:T(8,128)(2,1)S(1)} collective-permute-done((bf16[128,4096]{1,0:T(8,128)(2,1)S(1)}, bf16[128,4096]{1,0:T(8,128)(2,1)S(1)}, u32[]{:S(2)}, u32[]{:S(2)}) %collective-permute-start.1) | collective-permute-done | bytes 1048608 | tf_op jit(solution)/shard_map/ppermute | solution.py:12
  407.6 4.8 bitcast_dynamic-update-slice_fusion.4
  460.9 4.8 conditional.5
  476.4 72.0 %all-reduce.8.cloned.1.call-done = bf16[128,4096]{1,0:T(8,128)(2,1)} async-done(((bf16[128,4096]{1,0:T(8,128)(2,1)}), bf16[128,4096]{1,0:T(8,128)(2,1)}) %all-reduce.8.cloned.1.call-update) | async-done | bytes 1048592 | tf_op jit(solution)/shard_map/psum | solution.py:169
  558.3 12.4 %collective-permute-done.2 = bf16[128,4096]{1,0:T(8,128)(2,1)S(1)} collective-permute-done((bf16[128,4096]{1,0:T(8,128)(2,1)S(1)}, bf16[128,4096]{1,0:T(8,128)(2,1)S(1)}, u32[]{:S(2)}, u32[]{:S(2)}) %collective-permute-start.2) | collective-permute-done | bytes 1048608 | tf_op jit(solution)/shard_map/ppermute | solution.py:12
  570.7 4.8 bitcast_dynamic-update-slice_fusion.3
  604.4 5.7 convolution_bitcast_fusion.1
  610.1 5.7 convolution_bitcast_fusion.5
  615.8 5.7 convolution_bitcast_fusion.2
  621.5 5.7 convolution_bitcast_fusion.6
  629.2 5.9 convolution_bitcast_fusion
  635.1 5.7 convolution_bitcast_fusion.4
  654.0 5.7 convolution_bitcast_fusion.3
  662.1 5.8 convolution_bitcast_fusion.7
  667.9 31.8 %psum.31 = f32[2]{0:T(128)S(1)} all-reduce(f32[2]{0:T(128)S(1)} %and_select_fusion.3), channel_id=1, replica_groups=mesh['section'=2,'dp'=8,'mp'=8] {'section','mp'}, use_global_device_ids=true, to_apply=%region_37.38 | all-reduce | flops 2 | bytes 16 | tf_op jit(solution)/shard_map/psum | solution.py:172
  700.3 28.8 %fusion.33 = bf16[4096,4,512]{2,0,1:T(8,128)(2,1)} fusion(f32[4096,1,512]{2,0,1:T(8,128)} %convolution_bitcast_fusion.4, f32[4096,1,512]{2,0,1:T(8,128)} %convolution_bitcast_fusion.5, f32[4096,1,512]{2,0,1:T(8,128)} %convolution_bitcast_fusion.6, f32[4096,1,512]{2,0,1:T(8,128)} %convolution_bitcast_fusion.7, f32[4096,1,512]{2,0,1:T(8,128)} %convolution_bitcast_fusion, ...), kind=kLoop, calls=%fused_computation.37 | loop fusion | flops 83886080 | bytes 83886088 | tf_op jit(solution)/shard_map/convert_element_type | solution.py:202
  729.1 100.7 %reduce-scatter.2.cloned.1.call-done = bf16[512,4,512]{2,0,1:T(8,128)(2,1)} async-done(((bf16[4096,4,512]{2,0,1:T(8,128)(2,1)}), bf16[512,4,512]{2,0,1:T(8,128)(2,1)}) %reduce-scatter.2.cloned.1.call-update) | async-done | bytes 2097168 | tf_op jit(solution)/shard_map/reduce_scatter | solution.py:201
  (314 shorter events, 304.8 us)
Async XLA Ops:
  7.2 92.3 %all-gather.2.cloned.1.call-start = ((), (), s32[]{:S(2)}) async-start(), calls=%async_computation.1 | async-start | bytes 18874368 | tf_op jit(solution)/shard_map/all_gather | solution.py:94
  10.6 200.7 %all-reduce.4.cloned.1.call-start = ((), (), s32[]{:S(2)}) async-start(), calls=%async_computation.2 | async-start | bytes 2097152 | tf_op jit(solution)/shard_map/psum | solution.py:169
  21.3 86.0 %copy-start.38 = (f32[128]{0:T(128)}, f32[128]{0:T(128)S(1)}, u32[]{:S(2)}) copy-start(f32[128]{0:T(128)S(1)} %add_rsqrt_fusion.3) | copy-start | bytes 1540
  135.6 250.2 %all-reduce.6.cloned.1.call-start = ((), (), s32[]{:S(2)}) async-start(), calls=%async_computation.3 | async-start | bytes 2097152 | tf_op jit(solution)/shard_map/psum | solution.py:169
  224.9 20.6 %collective-permute-start = (bf16[128,4096]{1,0:T(8,128)(2,1)}, bf16[128,4096]{1,0:T(8,128)(2,1)}, u32[]{:S(2)}, u32[]{:S(2)}) collective-permute-start(bf16[128,4096]{1,0:T(8,128)(2,1)} %get-tuple-element.111), channel_id=1, source_target_pairs={{0,64},{64,0},{1,65},{65,1},{2,66},{66,2},{3,67},{67,3},{4,68},{68... | collective-permute-start | bytes 3145736 | tf_op jit(solution)/shard_map/ppermute | solution.py:12
  303.9 244.5 %all-reduce.8.cloned.1.call-start = ((), (), s32[]{:S(2)}) async-start(), calls=%async_computation.4 | async-start | bytes 2097152 | tf_op jit(solution)/shard_map/psum | solution.py:169
  304.7 7.4 copy-start.22
  306.3 7.3 copy-start.21
  387.3 20.3 %collective-permute-start.1 = (bf16[128,4096]{1,0:T(8,128)(2,1)S(1)}, bf16[128,4096]{1,0:T(8,128)(2,1)S(1)}, u32[]{:S(2)}, u32[]{:S(2)}) collective-permute-start(bf16[128,4096]{1,0:T(8,128)(2,1)S(1)} %fusion.67), channel_id=1, source_target_pairs={{0,64},{64,0},{1,65},{65,1},{2,66},{66,2},{3,67},{67,3},{4,68},{68... | collective-permute-start | bytes 3145736 | tf_op jit(solution)/shard_map/ppermute | solution.py:12
  392.4 15.2 %copy-start.4 = (bf16[2,128,4096]{2,1,0:T(8,128)(2,1)S(1)}, bf16[2,128,4096]{2,1,0:T(8,128)(2,1)}, u32[]{:S(2)}) copy-start(bf16[2,128,4096]{2,1,0:T(8,128)(2,1)} %param.15) | copy-start | bytes 6291460
  392.4 15.2 %copy-start.42 = (f32[128]{0:T(128)S(1)}, f32[128]{0:T(128)}, u32[]{:S(2)}) copy-start(f32[128]{0:T(128)} %add_rsqrt_fusion.1) | copy-start | bytes 1540
  392.4 15.2 %copy-start.46 = (bf16[128]{0:T(256)(128)(2,1)S(1)}, bf16[128]{0:T(256)(128)(2,1)}, u32[]{:S(2)}) copy-start(bf16[128]{0:T(256)(128)(2,1)} %compare_convert_fusion.1) | copy-start | bytes 772
  465.7 364.2 %reduce-scatter.2.cloned.1.call-start = ((), (), s32[]{:S(2)}) async-start(), calls=%async_computation.5 | async-start | bytes 18874368 | tf_op jit(solution)/shard_map/reduce_scatter | solution.py:201
  466.3 7.0 copy-start.24
  466.3 8.5 %copy-start.23 = (bf16[1,128,512]{2,1,0:T(8,128)(2,1)S(1)}, bf16[1,128,512]{2,1,0:T(8,128)(2,1)}, u32[]{:S(2)}) copy-start(bf16[1,128,512]{2,1,0:T(8,128)(2,1)} %copy.138) | copy-start | bytes 393220
  550.0 20.7 %collective-permute-start.2 = (bf16[128,4096]{1,0:T(8,128)(2,1)S(1)}, bf16[128,4096]{1,0:T(8,128)(2,1)S(1)}, u32[]{:S(2)}, u32[]{:S(2)}) collective-permute-start(bf16[128,4096]{1,0:T(8,128)(2,1)S(1)} %fusion.77), channel_id=1, source_target_pairs={{0,64},{64,0},{1,65},{65,1},{2,66},{66,2},{3,67},{67,3},{4,68},{68... | collective-permute-start | bytes 3145736 | tf_op jit(solution)/shard_map/ppermute | solution.py:12
  555.5 15.2 %copy-start.5 = (bf16[2,128,4096]{2,1,0:T(8,128)(2,1)S(1)}, bf16[2,128,4096]{2,1,0:T(8,128)(2,1)}, u32[]{:S(2)}) copy-start(bf16[2,128,4096]{2,1,0:T(8,128)(2,1)} %param.15) | copy-start | bytes 6291460
  555.5 15.2 %copy-start.41 = (f32[128]{0:T(128)S(1)}, f32[128]{0:T(128)}, u32[]{:S(2)}) copy-start(f32[128]{0:T(128)} %add_rsqrt_fusion) | copy-start | bytes 1540
  555.5 15.2 %copy-start.45 = (bf16[128]{0:T(256)(128)(2,1)S(1)}, bf16[128]{0:T(256)(128)(2,1)}, u32[]{:S(2)}) copy-start(bf16[128]{0:T(256)(128)(2,1)} %compare_convert_fusion) | copy-start | bytes 772
  579.5 6.4 copy-start.30
  585.9 7.0 copy-start.9
  589.5 9.8 %copy-start.11 = (f32[1,8,128,128]{2,3,1,0:T(8,128)S(1)}, f32[1,8,128,128]{2,3,1,0:T(8,128)}, u32[]{:S(2)}) copy-start(f32[1,8,128,128]{2,3,1,0:T(8,128)} %constant_dynamic-slice_fusion.13) | copy-start | bytes 1572868
  635.1 9.2 %copy-start.20 = (bf16[8,64,128]{2,1,0:T(8,128)(2,1)S(1)}, bf16[8,64,128]{2,1,0:T(8,128)(2,1)}, u32[]{:S(2)}) copy-start(bf16[8,64,128]{2,1,0:T(8,128)(2,1)} %copy-done.19) | copy-start | bytes 393220
  699.7 29.4 %copy-start.40 = (f32[2]{0:T(128)}, f32[2]{0:T(128)S(1)}, u32[]{:S(2)}) copy-start(f32[2]{0:T(128)S(1)} %add_divide_fusion) | copy-start | bytes 28
  (33 other events, 119.0 us)
Sparse Core Ops, SparseCore 0:
  10.7 88.7 all-gather.1
  135.7 75.4 all-reduce.3
  304.0 81.6 all-reduce.5
  465.8 82.5 all-reduce.7
  729.2 100.5 reduce-scatter.1
where the time goes:
time: 857 us; the launch traced here: 846 us
  waiting for transfers between devices  395 us (46%)
  matrix products  202 us (24%)
  other arithmetic  95.5 us (11%)
  local copies, waits for them, and re-layouts  91.1 us (11%)
  blocking collectives  31.8 us (4%)
  between operations  22.1 us (3%)
    psum x3, waiting for transfers between devices, per_device(): lax.psum(relay_term.astype(jnp.bfloat16), 'mp').astype(jnp.float32)  206 us
    reduce_scatter x1, waiting for transfers between devices, per_device(): lax.psum_scatter(totals.astype(jnp.bfloat16), 'dp', scatter_dimension=0,...  101 us
    all_gather x1, waiting for transfers between devices, per_device(): gathered = lax.all_gather(weights, 'dp', axis=1, tiled=True)[0]  60.7 us
    dot_general x16, matrix products, project(): jnp.dot(left, right, preferred_element_type=jnp.float32)  55 us
    dynamic_update_slice x25, other arithmetic, put_row(): lax.dynamic_update_index_in_dim(buffer, jnp.where(valid, value, current),...  45.1 us
    dot_general x28, matrix products, gram(): return jnp.dot(matrix, matrix.T, preferred_element_type=jnp.float32)  42.7 us
    dynamic_slice x35, local copies, waits for them, and re-layouts, get_row(): return lax.dynamic_index_in_dim(buffer, index, 0, keepdims=False)  37.2 us
    psum x1, blocking collectives, per_device(): sq_norm = lax.psum(norm_parts, ('section', 'mp'))  31.8 us
  transfers between devices with their start and end apart: 8, of which 8 were waited for; matrix products, arithmetic and copies ran while one was open for 10% of the time, Pallas kernels for 0%

commit v1 on v0

--- a/solution.py
+++ b/solution.py
@@ -6,6 +6,11 @@
 D = 4096
 HEADS = 64
 HEAD = 64
+
+
+def _mix_matrix(local):
+    w2 = jnp.stack([local for _ in range(lax.axis_size("dp"))])
+    return jnp.concatenate(lax.all_to_all(w2, "dp", 0, 0), 1)
 
 
 def from_partner(x, axis, distance):
@@ -91,7 +96,7 @@
     micro_count = inputs.shape[1]
     seq_len = inputs.shape[2]
     width = inputs.shape[3]
-    gathered = lax.all_gather(weights, "dp", axis=1, tiled=True)[0]
+    gathered = _mix_matrix(weights)[0]
     inner_dev = gathered.shape[2]
     own_inputs = inputs[0]
     gain_row = norm_gains[0]

time: 857 us -> 970 us (1.13)
  waiting for transfers between devices: 395 us -> 490 us
  local copies, waits for them, and re-layouts: 91.1 us -> 106 us
    all_to_all x0 -> x1, waiting for transfers between devices: none -> 156 us  [_mix_matrix(): return jnp.concatenate(lax.all_to_all(w2, 'dp', 0, 0), 1)]
    all_gather x1 -> x0, waiting for transfers between devices: 60.7 us -> none  [per_device(): gathered = lax.all_gather(weights, 'dp', axis=1, tiled=True)[0]]
  transfers between devices with their start and end apart: 8 -> 8, of which waited for: 8 -> 8; matrix products, arithmetic and copies ran while one was open for 10% -> 9% of each run, Pallas kernels for 0% -> 0%
where the time goes in v1:
time: 970 us; the launch traced here: 959 us
  waiting for transfers between devices  490 us (51%)
  matrix products  198 us (20%)
  local copies, waits for them, and re-layouts  106 us (11%)
  other arithmetic  95.7 us (10%)
  blocking collectives  31.7 us (3%)
  between operations  22.1 us (2%)
  starting transfers between devices  15.5 us (2%)
    psum x3, waiting for transfers between devices, per_device(): lax.psum(relay_term.astype(jnp.bfloat16), 'mp').astype(jnp.float32)  206 us
    all_to_all x1, waiting for transfers between devices, _mix_matrix(): return jnp.concatenate(lax.all_to_all(w2, 'dp', 0, 0), 1)  156 us
    reduce_scatter x1, waiting for transfers between devices, per_device(): lax.psum_scatter(totals.astype(jnp.bfloat16), 'dp', scatter_dimension=0,...  101 us
    dot_general x16, matrix products, project(): jnp.dot(left, right, preferred_element_type=jnp.float32)  50.9 us
    dynamic_update_slice x25, other arithmetic, put_row(): lax.dynamic_update_index_in_dim(buffer, jnp.where(valid, value, current),...  45.1 us
    dot_general x28, matrix products, gram(): return jnp.dot(matrix, matrix.T, preferred_element_type=jnp.float32)  42.5 us
    dynamic_slice x35, local copies, waits for them, and re-layouts, get_row(): return lax.dynamic_index_in_dim(buffer, index, 0, keepdims=False)  37.2 us
    psum x1, blocking collectives, per_device(): sq_norm = lax.psum(norm_parts, ('section', 'mp'))  31.7 us
  transfers between devices with their start and end apart: 8, of which 8 were waited for; matrix products, arithmetic and copies ran while one was open for 9% of the time, Pallas kernels for 0%

profile of v1, /device:TPU:1, one launch (start us, length us, event | category | flops | bytes accessed | tf_op | source)
XLA Modules:
  0.0 958.8 jit_solution(9097772734429967791)
XLA Ops:
  9.2 5.9 stack.41
  15.1 7.1 all-to-all-start
  49.7 155.9 %all-to-all-done = bf16[8,1,512,4,512]{4,2,3,1,0:T(8,128)(2,1)} async-done(((bf16[8,1,512,4,512]{4,2,3,1,0:T(8,128)(2,1)}), bf16[8,1,512,4,512]{4,2,3,1,0:T(8,128)(2,1)}, u32[]{:S(2)}, u32[]{:S(2)}) %all-to-all-start) | async-done | bytes 16777248 | tf_op jit(solution)/shard_map/all_to_all | solution.py:13
  205.6 8.5 copy.147
  261.1 63.2 %all-reduce.4.cloned.1.call-done = bf16[128,4096]{1,0:T(8,128)(2,1)} async-done(((bf16[128,4096]{1,0:T(8,128)(2,1)}), bf16[128,4096]{1,0:T(8,128)(2,1)}) %all-reduce.4.cloned.1.call-update) | async-done | bytes 1048592 | tf_op jit(solution)/shard_map/psum | solution.py:174
  358.5 6.0 bitcast_dynamic-update-slice_fusion.5
  412.0 4.9 conditional.4
  428.2 70.6 %all-reduce.6.cloned.1.call-done = bf16[128,4096]{1,0:T(8,128)(2,1)} async-done(((bf16[128,4096]{1,0:T(8,128)(2,1)}), bf16[128,4096]{1,0:T(8,128)(2,1)}) %all-reduce.6.cloned.1.call-update) | async-done | bytes 1048592 | tf_op jit(solution)/shard_map/psum | solution.py:174
  508.3 12.4 %collective-permute-done.1 = bf16[128,4096]{1,0:T(8,128)(2,1)S(1)} collective-permute-done((bf16[128,4096]{1,0:T(8,128)(2,1)S(1)}, bf16[128,4096]{1,0:T(8,128)(2,1)S(1)}, u32[]{:S(2)}, u32[]{:S(2)}) %collective-permute-start.1) | collective-permute-done | bytes 1048608 | tf_op jit(solution)/shard_map/ppermute | solution.py:17
  520.7 4.8 bitcast_dynamic-update-slice_fusion.4
  589.5 72.1 %all-reduce.8.cloned.1.call-done = bf16[128,4096]{1,0:T(8,128)(2,1)} async-done(((bf16[128,4096]{1,0:T(8,128)(2,1)}), bf16[128,4096]{1,0:T(8,128)(2,1)}) %all-reduce.8.cloned.1.call-update) | async-done | bytes 1048592 | tf_op jit(solution)/shard_map/psum | solution.py:174
  671.4 12.4 %collective-permute-done.2 = bf16[128,4096]{1,0:T(8,128)(2,1)S(1)} collective-permute-done((bf16[128,4096]{1,0:T(8,128)(2,1)S(1)}, bf16[128,4096]{1,0:T(8,128)(2,1)S(1)}, u32[]{:S(2)}, u32[]{:S(2)}) %collective-permute-start.2) | collective-permute-done | bytes 1048608 | tf_op jit(solution)/shard_map/ppermute | solution.py:17
  683.8 4.8 bitcast_dynamic-update-slice_fusion.3
  717.5 5.7 convolution_bitcast_fusion.1
  723.2 5.7 convolution_bitcast_fusion.5
  729.0 5.7 convolution_bitcast_fusion.2
  734.7 5.7 convolution_bitcast_fusion.6
  742.4 5.8 convolution_bitcast_fusion
  748.2 5.7 convolution_bitcast_fusion.4
  767.1 5.7 convolution_bitcast_fusion.3
  775.2 5.8 convolution_bitcast_fusion.7
  781.0 31.7 %psum.31 = f32[2]{0:T(128)S(1)} all-reduce(f32[2]{0:T(128)S(1)} %and_select_fusion.3), channel_id=1, replica_groups=mesh['section'=2,'dp'=8,'mp'=8] {'section','mp'}, use_global_device_ids=true, to_apply=%region_37.38 | all-reduce | flops 2 | bytes 16 | tf_op jit(solution)/shard_map/psum | solution.py:177
  813.4 28.8 %fusion.33 = bf16[4096,4,512]{2,0,1:T(8,128)(2,1)} fusion(f32[4096,1,512]{2,0,1:T(8,128)} %convolution_bitcast_fusion.4, f32[4096,1,512]{2,0,1:T(8,128)} %convolution_bitcast_fusion.5, f32[4096,1,512]{2,0,1:T(8,128)} %convolution_bitcast_fusion.6, f32[4096,1,512]{2,0,1:T(8,128)} %convolution_bitcast_fusion.7, f32[4096,1,512]{2,0,1:T(8,128)} %convolution_bitcast_fusion, ...), kind=kLoop, calls=%fused_computation.37 | loop fusion | flops 83886080 | bytes 83886088 | tf_op jit(solution)/shard_map/convert_element_type | solution.py:207
  842.2 100.8 %reduce-scatter.2.cloned.1.call-done = bf16[512,4,512]{2,0,1:T(8,128)(2,1)} async-done(((bf16[4096,4,512]{2,0,1:T(8,128)(2,1)}), bf16[512,4,512]{2,0,1:T(8,128)(2,1)}) %reduce-scatter.2.cloned.1.call-update) | async-done | bytes 2097168 | tf_op jit(solution)/shard_map/reduce_scatter | solution.py:206
  (315 shorter events, 315.2 us)
Async XLA Ops:
  15.1 7.2 copy-start.39
  15.1 7.2 copy-start.44
  15.1 8.6 copy-start.1
  15.1 190.5 %all-to-all-start = ((bf16[8,1,512,4,512]{4,2,3,1,0:T(8,128)(2,1)}), bf16[8,1,512,4,512]{4,2,3,1,0:T(8,128)(2,1)}, u32[]{:S(2)}, u32[]{:S(2)}) async-start(bf16[8,1,512,4,512]{4,2,3,1,0:T(8,128)(2,1)} %stack.41), calls=%async_computation | async-start | bytes 33554432 | tf_op jit(solution)/shard_map/all_to_all | solution.py:13
  22.2 302.1 %all-reduce.4.cloned.1.call-start = ((), (), s32[]{:S(2)}) async-start(), calls=%async_computation.2 | async-start | bytes 2097152 | tf_op jit(solution)/shard_map/psum | solution.py:174
  205.6 8.5 copy-start.5
  248.4 250.4 %all-reduce.6.cloned.1.call-start = ((), (), s32[]{:S(2)}) async-start(), calls=%async_computation.3 | async-start | bytes 2097152 | tf_op jit(solution)/shard_map/psum | solution.py:174
  337.9 20.6 %collective-permute-start = (bf16[128,4096]{1,0:T(8,128)(2,1)}, bf16[128,4096]{1,0:T(8,128)(2,1)}, u32[]{:S(2)}, u32[]{:S(2)}) collective-permute-start(bf16[128,4096]{1,0:T(8,128)(2,1)} %get-tuple-element.113), channel_id=1, source_target_pairs={{0,64},{64,0},{1,65},{65,1},{2,66},{66,2},{3,67},{67,3},{4,68},{68... | collective-permute-start | bytes 3145736 | tf_op jit(solution)/shard_map/ppermute | solution.py:17
  416.9 244.6 %all-reduce.8.cloned.1.call-start = ((), (), s32[]{:S(2)}) async-start(), calls=%async_computation.4 | async-start | bytes 2097152 | tf_op jit(solution)/shard_map/psum | solution.py:174
  417.7 7.4 copy-start.24
  419.3 7.3 copy-start.23
  500.3 20.3 %collective-permute-start.1 = (bf16[128,4096]{1,0:T(8,128)(2,1)S(1)}, bf16[128,4096]{1,0:T(8,128)(2,1)S(1)}, u32[]{:S(2)}, u32[]{:S(2)}) collective-permute-start(bf16[128,4096]{1,0:T(8,128)(2,1)S(1)} %fusion.67), channel_id=1, source_target_pairs={{0,64},{64,0},{1,65},{65,1},{2,66},{66,2},{3,67},{67,3},{4,68},{68... | collective-permute-start | bytes 3145736 | tf_op jit(solution)/shard_map/ppermute | solution.py:17
  505.5 15.2 %copy-start.6 = (bf16[2,128,4096]{2,1,0:T(8,128)(2,1)S(1)}, bf16[2,128,4096]{2,1,0:T(8,128)(2,1)}, u32[]{:S(2)}) copy-start(bf16[2,128,4096]{2,1,0:T(8,128)(2,1)} %param.15) | copy-start | bytes 6291460
  505.5 15.2 %copy-start.42 = (f32[128]{0:T(128)S(1)}, f32[128]{0:T(128)}, u32[]{:S(2)}) copy-start(f32[128]{0:T(128)} %add_rsqrt_fusion.1) | copy-start | bytes 1540
  505.5 15.2 %copy-start.46 = (bf16[128]{0:T(256)(128)(2,1)S(1)}, bf16[128]{0:T(256)(128)(2,1)}, u32[]{:S(2)}) copy-start(bf16[128]{0:T(256)(128)(2,1)} %compare_convert_fusion.1) | copy-start | bytes 772
  578.7 364.3 %reduce-scatter.2.cloned.1.call-start = ((), (), s32[]{:S(2)}) async-start(), calls=%async_computation.5 | async-start | bytes 18874368 | tf_op jit(solution)/shard_map/reduce_scatter | solution.py:206
  579.4 8.5 copy-start.25
  663.1 20.7 %collective-permute-start.2 = (bf16[128,4096]{1,0:T(8,128)(2,1)S(1)}, bf16[128,4096]{1,0:T(8,128)(2,1)S(1)}, u32[]{:S(2)}, u32[]{:S(2)}) collective-permute-start(bf16[128,4096]{1,0:T(8,128)(2,1)S(1)} %fusion.77), channel_id=1, source_target_pairs={{0,64},{64,0},{1,65},{65,1},{2,66},{66,2},{3,67},{67,3},{4,68},{68... | collective-permute-start | bytes 3145736 | tf_op jit(solution)/shard_map/ppermute | solution.py:17
  668.6 15.2 %copy-start.7 = (bf16[2,128,4096]{2,1,0:T(8,128)(2,1)S(1)}, bf16[2,128,4096]{2,1,0:T(8,128)(2,1)}, u32[]{:S(2)}) copy-start(bf16[2,128,4096]{2,1,0:T(8,128)(2,1)} %param.15) | copy-start | bytes 6291460
  668.6 15.2 %copy-start.41 = (f32[128]{0:T(128)S(1)}, f32[128]{0:T(128)}, u32[]{:S(2)}) copy-start(f32[128]{0:T(128)} %add_rsqrt_fusion) | copy-start | bytes 1540
  668.6 15.2 %copy-start.45 = (bf16[128]{0:T(256)(128)(2,1)S(1)}, bf16[128]{0:T(256)(128)(2,1)}, u32[]{:S(2)}) copy-start(bf16[128]{0:T(256)(128)(2,1)} %compare_convert_fusion) | copy-start | bytes 772
  702.6 9.8 %copy-start.13 = (f32[1,8,128,128]{2,3,1,0:T(8,128)S(1)}, f32[1,8,128,128]{2,3,1,0:T(8,128)}, u32[]{:S(2)}) copy-start(f32[1,8,128,128]{2,3,1,0:T(8,128)} %constant_dynamic-slice_fusion.13) | copy-start | bytes 1572868
  748.2 9.2 copy-start.22
  812.8 29.4 %copy-start.40 = (f32[2]{0:T(128)}, f32[2]{0:T(128)S(1)}, u32[]{:S(2)}) copy-start(f32[2]{0:T(128)S(1)} %add_divide_fusion) | copy-start | bytes 28
  (33 other events, 139.2 us)
Sparse Core Ops, SparseCore 0:
  248.5 75.7 all-reduce.3
  417.1 81.7 all-reduce.5
  578.9 82.6 all-reduce.7
  842.4 100.5 reduce-scatter.1
